TPU v7x, 32 devices: a whole 2x2x4 slice. The times are simulated.
32 devices in a mesh: layer: 8 (over y, x, core), dp: 4 (over z).
Axes of the slice: x: 2, y: 2, z: 4, core: 2. Of those that a mesh axis runs over, the one named last changes fastest.
Arguments:
- images: float32 [8, 16, 16, 128], P('dp'), may hold values from -6 to 6
- weights: bfloat16 [32, 3, 3, 128, 128], P('layer'), may hold values from -0.1875 to 0.1875
- biases: float32 [32, 128], P('layer'), may hold values from -3 to 3
- end_grad: float32 [8, 16, 16, 128], P('dp'), may hold values from -6 to 6
Outputs:
- interval_ends: float32 [8, 8, 16, 16, 128], P('layer', 'dp')
- start_adjoint: float32 [8, 8, 16, 16, 128], P('layer', 'dp')
- weight_grad: float32 [32, 3, 3, 128, 128], P('layer')
- bias_grad: float32 [32, 128], P('layer')
All inputs are finite; a program needn't handle non-finite values.
Results may differ from a plain program's by a relative error of at most 0.012.
The roundings to bfloat16 on the way count: a program that leaves them out, or rounds other values in their place, can miss the bound.
Values sent between devices are 32-bit elements; how exact they have to be, the bound alone decides.
A program may use at most 128 MiB of HBM per device.

v0:
```python
import functools

import jax
import jax.numpy as jnp
from jax import lax
from jax.experimental import pallas as pl
from jax.experimental.pallas import tpu as pltpu
from jax.sharding import PartitionSpec as P

step_size = 0.25
MESH = pl.DeviceIdType.MESH
low = jnp.bfloat16


def dot(a, b, contract=((1,), (0,))):
    return lax.dot_general(a, b, (contract, ((), ())), preferred_element_type=jnp.float32)


NT = ((1,), (1,))
TN = ((0,), (0,))


def kernel(
    dims,
    images_in,
    weights_in,
    biases_in,
    end_grad_in,
    both_out,
    wg_out,
    bg_out,
    images,
    weights,
    biases,
    end_grad,
    load_sems,
    flipped,
    window,
    maps,
    states_low,
    slopes,
    states_all,
    adj_all,
    residue,
    gathered,
    spread,
    error,
    map_send,
    map_recv,
    hand_send,
    out_send,
    out_recv,
    back_send,
    back_recv,
    right_send,
    left_send,
    line_recv,
):
    groups, parts, count, height, width, images_all = dims
    rows, channels = images_in.shape
    blocks = weights_in.shape[0]
    share = rows // groups
    me = lax.axis_index("layer")
    z = lax.axis_index("dp")
    not_first = z > 0
    not_last = z < parts - 1

    def others(body):
        def step(ahead, _):
            body(ahead, lax.rem(me + ahead, groups))
            return 0

        lax.fori_loop(1, groups, step, 0)

    loads = [
        pltpu.make_async_copy(source, target, load_sems.at[i])
        for i, (source, target) in enumerate(
            ((weights_in, weights), (images_in, images), (biases_in, biases), (end_grad_in, end_grad))
        )
    ]
    for load in loads:
        load.start()
    barrier = pltpu.get_barrier_semaphore()
    others(lambda ahead, to: pl.semaphore_signal(barrier, inc=1, device_id={"layer": to}, device_id_type=MESH))

    @pl.when(not_first)
    def _():
        pl.semaphore_signal(barrier, inc=1, device_id={"dp": z - 1}, device_id_type=MESH)

    @pl.when(not_last)
    def _():
        pl.semaphore_signal(barrier, inc=1, device_id={"dp": z + 1}, device_id_type=MESH)

    loads[0].wait()
    centre = slice(4 * channels, 5 * channels)
    total = weights[0, centre, :].astype(jnp.float32)
    for n in range(1, blocks):
        total = total + weights[n, centre, :].astype(jnp.float32)
    maps[me] = step_size * total

    neighbours = jnp.where(not_first, 1, 0) + jnp.where(not_last, 1, 0)
    pl.semaphore_wait(barrier, groups - 1 + neighbours)

    def map_copy(slot, to):
        return pltpu.make_async_remote_copy(
            src_ref=maps.at[slot],
            dst_ref=maps.at[slot],
            send_sem=map_send.at[to],
            recv_sem=map_recv.at[slot],
            device_id={"layer": to},
            device_id_type=MESH,
        )

    last = groups - 1
    after = lax.rem(me + 1, groups)
    before = lax.rem(me + last, groups)
    pair = 2 if groups % 2 == 0 else 1
    partner = me + 1 - 2 * lax.rem(me, 2) if pair == 2 else me

    def same_side(body):
        def step(ahead, _):
            body(lax.rem(me + pair * ahead, groups))
            return 0

        lax.fori_loop(1, groups // pair, step, 0)

    map_copy(me, after).start()
    if pair == 2:

        @pl.when(partner != after)
        def _():
            map_copy(me, partner).start()

    def send_map(to):
        if pair == 1:

            @pl.when(to != after)
            def _():
                map_copy(me, to).start()

        else:
            map_copy(me, to).start()

    same_side(send_map)

    def hand_copy(slot):
        return pltpu.make_async_remote_copy(
            src_ref=maps.at[slot],
            dst_ref=maps.at[slot],
            send_sem=hand_send.at[slot],
            recv_sem=map_recv.at[slot],
            device_id={"layer": partner},
            device_id_type=MESH,
        )

    def is_handed(slot):
        return lax.rem(slot + 1, groups) != partner

    def hand_on(slot):
        @pl.when((slot != before) | (me == 0))
        def _():
            map_copy(slot, me).wait_recv()

        if pair == 2:

            @pl.when(is_handed(slot))
            def _():
                hand_copy(slot).start()

    for load in loads[1:]:
        load.wait()

    zero_row = jnp.zeros((count, 1, width, 3 * channels), low)
    window[:, 0:1] = zero_row
    window[:, height + 1 : height + 2] = zero_row

    def prepare(n, _):
        for tap in range(9):
            flipped[n, :, tap * channels : (tap + 1) * channels] = weights[
                n, (8 - tap) * channels : (9 - tap) * channels, :
            ]
        wg_out[n] = jnp.zeros(wg_out.shape[1:], jnp.float32)
        return 0

    lax.fori_loop(0, blocks, prepare, 0)
    bg_out[...] = jnp.zeros(bg_out.shape, jnp.float32)

    column = lax.rem(lax.broadcasted_iota(jnp.int32, (rows, channels), 0), width)

    def patches(field):
        size = field.shape[0]
        some = size // (height * width)
        place = column[:size]
        left = jnp.where(place == 0, 0.0, pltpu.roll(field, 1, 0))
        right = jnp.where(place == width - 1, 0.0, pltpu.roll(field, size - 1, 0))
        shape = (some, height, width, channels)
        window[:some, 1 : height + 1, :, 0:channels] = left.astype(low).reshape(shape)
        window[:some, 1 : height + 1, :, channels : 2 * channels] = field.astype(low).reshape(shape)
        window[:some, 1 : height + 1, :, 2 * channels : 3 * channels] = right.astype(low).reshape(shape)
        return jnp.concatenate(
            [window[:some, i : i + height].reshape(size, 3 * channels) for i in range(3)], axis=1
        )

    def apply_map(field, slot):
        return field + dot(field.astype(low), maps[slot].astype(low))

    def apply_flipped(field, slot):
        return field + dot(field.astype(low), maps[slot].astype(low), NT)

    def advance(n, state):
        return state + step_size * jnp.tanh(dot(patches(state), weights[n]) + biases[pl.ds(n, 1), :])

    def trajectory(part, state):
        def step(n, state):
            states_low[n, part] = state.astype(low)
            activation = jnp.tanh(dot(patches(state), weights[n]) + biases[pl.ds(n, 1), :])
            slopes[n, part] = activation
            return state + step_size * activation

        return lax.fori_loop(0, blocks, step, state)

    def change_of(n, part, adjoint, at=0):
        slope = slopes[n, part, at : at + adjoint.shape[0]]
        return step_size * (1.0 - slope * slope) * adjoint

    def retreat(part, adjoint):
        def step(i, adjoint):
            n = blocks - 1 - i
            return adjoint + dot(patches(change_of(n, part, adjoint)), flipped[n], NT)

        return lax.fori_loop(0, blocks, step, adjoint)

    divisor = 1.0 / images_all

    def sweep(part, adjoint, at=0):
        def step(i, adjoint):
            n = blocks - 1 - i
            change = change_of(n, part, adjoint, at)
            bg_out[pl.ds(n, 1), :] += jnp.sum(change, axis=0, keepdims=True) * divisor
            spots = patches(change)
            adjoint = adjoint + dot(spots, flipped[n], NT)
            grads = dot(states_low[n, part, at : at + adjoint.shape[0]], spots, TN) * divisor
            for tap in range(9):
                wg_out[n, (8 - tap) * channels : (9 - tap) * channels, :] += grads[
                    :, tap * channels : (tap + 1) * channels
                ]
            return adjoint

        return lax.fori_loop(0, blocks, step, adjoint)

    def rows_of(slot):
        return pl.ds(pl.multiple_of(slot * share, share), share)

    def out_copy(phase, source, to):
        return pltpu.make_async_remote_copy(
            src_ref=residue.at[phase, rows_of(to)],
            dst_ref=gathered.at[phase, source],
            send_sem=out_send.at[phase, to],
            recv_sem=out_recv.at[phase, source],
            device_id={"layer": to},
            device_id_type=MESH,
        )

    def back_copy(phase, source, to):
        return pltpu.make_async_remote_copy(
            src_ref=spread.at[phase, to],
            dst_ref=error.at[phase, rows_of(source)],
            send_sem=back_send.at[phase, to],
            recv_sem=back_recv.at[phase, source],
            device_id={"layer": to},
            device_id_type=MESH,
        )

    def chain_start(phase, value):
        residue[phase] = value
        others(lambda ahead, to: out_copy(phase, me, to).start())
        gathered[phase, me] = residue[phase, rows_of(me)]

    def chain_scan(phase):
        def step(i, carried):
            k = i if phase == 0 else groups - 1 - i

            @pl.when(k != me)
            def _():
                spread[phase, k] = carried
                back_copy(phase, me, k).start()
                out_copy(phase, k, me).wait_recv()

            @pl.when(k == me)
            def _():
                error[phase, rows_of(me)] = carried

            mapped = apply_map(carried, k) if phase == 0 else apply_flipped(carried, k)
            return mapped + gathered[phase, k]

        lax.fori_loop(0, groups, step, jnp.zeros((share, channels), jnp.float32))

    def chain_finish(phase):
        others(lambda ahead, to: back_copy(phase, to, me).wait_recv())
        return error[phase]

    line = (states_all, adj_all)

    piece = rows // count

    def line_copy(which, block, part, to, sends):
        where = line[which].at[block, part * piece : (part + 1) * piece]
        return pltpu.make_async_remote_copy(
            src_ref=where,
            dst_ref=where,
            send_sem=sends.at[which, block, part],
            recv_sem=line_recv.at[which, block, part],
            device_id={"dp": to},
            device_id_type=MESH,
        )

    def go_right(which, block, part):
        @pl.when(not_last)
        def _():
            line_copy(which, block, part, z + 1, right_send).start()

    def go_left(which, block, part):
        @pl.when(not_first)
        def _():
            line_copy(which, block, part, z - 1, left_send).start()

    def line_start(which):
        for part in range(count):
            go_right(which, z, part)
            go_left(which, z, part)

    def line_round(which, away, pieces=range(count)):
        for part in pieces:

            @pl.when(z - away >= 0)
            def _():
                line_copy(which, z - away, part, z, right_send).wait_recv()
                go_right(which, z - away, part)

            @pl.when(z + away < parts)
            def _():
                line_copy(which, z + away, part, z, left_send).wait_recv()
                go_left(which, z + away, part)

    def nth_other(i):
        back_side = parts - 1 - z
        paired = jnp.where(z < back_side, z, back_side)
        near = i // 2 + 1
        near_part = jnp.where(i % 2 == 0, z - near, z + near)
        far = i - paired + 1
        far_part = jnp.where(z > back_side, z - far, z + far)
        return jnp.where(i < 2 * paired, near_part, far_part)

    def other_trajectory(i):
        part = nth_other(i)
        trajectory(part, states_all[part])

    start_image = images[...]

    @pl.when(me != 0)
    def _():
        map_copy(before, me).wait_recv()

    starts = jnp.where(me == 0, start_image, apply_map(start_image, jnp.where(me == 0, me, before)))
    relaxed = lax.fori_loop(0, blocks, advance, starts)
    chain_start(0, relaxed - apply_map(start_image, me))

    same_side(hand_on)

    def wait_map(ahead, source):
        @pl.when((lax.rem(source - me + groups, pair) != 0) & ((source != before) | (me == 0)))
        def _():
            map_copy(source, me).wait_recv()

    if pair == 2:
        others(wait_map)
    end = end_grad[...]
    ends_adj = jnp.where(me == last, end, apply_flipped(end, after))
    back = apply_flipped(end, me)
    chain_scan(0)
    corrected = starts + chain_finish(0)
    states_all[z] = corrected
    line_start(0)
    both_out[0] = trajectory(z, corrected)

    chain_start(1, retreat(z, ends_adj) - back)
    if parts > 1:
        line_round(0, 1)
        other_trajectory(0)
    chain_scan(1)
    if parts > 2:
        line_round(0, 2)
        other_trajectory(1)
    adjoint = ends_adj + chain_finish(1)
    adj_all[z] = adjoint
    line_start(1)
    both_out[1] = sweep(z, adjoint)
    for i in range(2, parts - 1):
        line_round(0, i + 1)
        other_trajectory(i)
    for i in range(parts - 2):
        line_round(1, i + 1)
        part = nth_other(i)
        sweep(part, adj_all[part])
    if parts > 1:
        part = nth_other(parts - 2)
        for i in range(count):
            line_round(1, parts - 1, (i,))
            sweep(part, adj_all[part, i * piece : (i + 1) * piece], i * piece)

    def map_sent(to):
        if pair == 1:

            @pl.when(to != after)
            def _():
                map_copy(me, to).wait_send()

        else:
            map_copy(me, to).wait_send()

            @pl.when(is_handed(to))
            def _():
                hand_copy(to).wait_send()

    map_copy(me, after).wait_send()
    if pair == 2:

        @pl.when(partner != after)
        def _():
            map_copy(me, partner).wait_send()

    same_side(map_sent)

    def sent(ahead, to):
        for phase in range(2):
            out_copy(phase, me, to).wait_send()
            back_copy(phase, me, to).wait_send()

    others(sent)
    for which in range(2):
        for away in range(parts):

            @pl.when((z - away >= 0) & not_last)
            def _():
                for part in range(count):
                    line_copy(which, z - away, part, z + 1, right_send).wait_send()

            @pl.when((z + away < parts) & not_first)
            def _():
                for part in range(count):
                    line_copy(which, z + away, part, z - 1, left_send).wait_send()


def shards(images, weights, biases, end_grad):
    groups = lax.axis_size("layer")
    parts = lax.axis_size("dp")
    count, height, width, channels = images.shape
    blocks = weights.shape[0]
    rows = count * height * width
    dims = (groups, parts, count, height, width, count * parts)
    f32 = jnp.float32
    share = rows // groups
    dma = pltpu.SemaphoreType.DMA
    vmem = pl.BlockSpec(memory_space=pltpu.VMEM)
    both, wg, bg = pl.pallas_call(
        functools.partial(kernel, dims),
        out_shape=(
            pltpu.VMEM((2, rows, channels), f32),
            pltpu.VMEM((blocks, 9 * channels, channels), f32),
            pltpu.VMEM((blocks, channels), f32),
        ),
        in_specs=[pl.BlockSpec(memory_space=pltpu.HBM)] * 4,
        out_specs=(vmem,) * 3,
        scratch_shapes=[
            pltpu.VMEM((rows, channels), f32),
            pltpu.VMEM((blocks, 9 * channels, channels), low),
            pltpu.VMEM((blocks, channels), f32),
            pltpu.VMEM((rows, channels), f32),
            dma((4,)),
            pltpu.VMEM((blocks, channels, 9 * channels), low),
            pltpu.VMEM((count, height + 2, width, 3 * channels), low),
            pltpu.VMEM((groups, channels, channels), f32),
            pltpu.VMEM((blocks, parts, rows, channels), low),
            pltpu.VMEM((blocks, parts, rows, channels), f32),
            pltpu.VMEM((parts, rows, channels), f32),
            pltpu.VMEM((parts, rows, channels), f32),
            pltpu.VMEM((2, rows, channels), f32),
            pltpu.VMEM((2, groups, share, channels), f32),
            pltpu.VMEM((2, groups, share, channels), f32),
            pltpu.VMEM((2, rows, channels), f32),
            dma((groups,)),
            dma((groups,)),
            dma((groups,)),
            dma((2, groups)),
            dma((2, groups)),
            dma((2, groups)),
            dma((2, groups)),
            dma((2, parts, count)),
            dma((2, parts, count)),
            dma((2, parts, count)),
        ],
        compiler_params=pltpu.CompilerParams(
            collective_id=0, has_side_effects=True, vmem_limit_bytes=61 << 20
        ),
    )(
        images.reshape(rows, channels),
        weights.reshape(blocks, 9 * channels, channels),
        biases,
        end_grad.reshape(rows, channels),
    )
    shape = (1,) + images.shape
    return (both[0].reshape(shape), both[1].reshape(shape), wg.reshape(weights.shape), bg)


def solution(mesh):
    in_specs = (
        P("dp", None, None, None),
        P("layer", None, None, None, None),
        P("layer", None),
        P("dp", None, None, None),
    )
    out_specs = (
        P("layer", "dp", None, None, None),
        P("layer", "dp", None, None, None),
        P("layer", None, None, None, None),
        P("layer", None),
    )
    return jax.shard_map(shards, mesh=mesh, in_specs=in_specs, out_specs=out_specs, check_vma=False)
```

profile of v0, /device:TPU:0, one launch (start us, length us, event | category | flops | bytes accessed | tf_op | source)
XLA Modules:
  0.0 59.3 jit_solution(13983924762610491863)
XLA Ops:
  0.6 55.9 %shard_map.75 = (f32[2,512,128]{2,1,0:T(8,128)S(1)}, f32[4,1152,128]{2,1,0:T(8,128)S(1)}, f32[4,128]{1,0:T(4,128)S(1)}) custom-call(f32[512,128]{1,0:T(8,128)} %bitcast.8, bf16[4,1152,128]{2,1,0:T(8,128)(2,1)} %bitcast.7, f32[4,128]{1,0:T(4,128)} %biases_in.1, f32[512,128]{1,0:T(8,128)} %bitcast.9), custom_call_target="tpu_custom_call" | custom-call | tf_op jit(solution)/shard_map/pallas_call | solution.py:465
  56.5 1.4 %copy.10 = f32[4,3,3,128,128]{4,3,2,1,0:T(8,128)} copy(f32[4,3,3,128,128]{4,3,2,1,0:T(8,128)S(1)} %bitcast.6) | data formatting | bytes 4718592
  57.9 0.8 %fusion = (f32[1,512,128]{2,1,0:T(8,128)}, f32[1,512,128]{2,1,0:T(8,128)}) fusion(f32[2,512,128]{2,1,0:T(8,128)S(1)} %get-tuple-element.7), kind=kLoop, calls=%fused_computation | loop fusion | bytes 1048576 | tf_op jit(solution)/shard_map/slice | solution.py:512
  58.7 0.6 copy.11
where the time goes:
time: 59.5 us; the launch traced here: 59.3 us
  Pallas kernels  55.9 us (94%)
  local copies, waits for them, and re-layouts  2.81 us (5%)
  between operations  0.64 us (1%)
    pallas_call x1, Pallas kernels, shards(): pl.pallas_call(functools.partial(kernel, dims), out_shape=(pltpu.VMEM((2,...  55.9 us
    unnamed x2, local copies, waits for them, and re-layouts  1.99 us

commit v1 on v0

--- a/solution.py
+++ b/solution.py
@@ -16,6 +16,7 @@
     return lax.dot_general(a, b, (contract, ((), ())), preferred_element_type=jnp.float32)
 
 
+NN = ((1,), (0,))
 NT = ((1,), (1,))
 TN = ((0,), (0,))
 
@@ -34,8 +35,10 @@
     biases,
     end_grad,
     load_sems,
-    flipped,
-    window,
+    ahead_pair,
+    ahead_edge,
+    back_pair,
+    back_edge,
     maps,
     states_low,
     slopes,
@@ -170,15 +173,27 @@
     for load in loads[1:]:
         load.wait()
 
-    zero_row = jnp.zeros((count, 1, width, 3 * channels), low)
-    window[:, 0:1] = zero_row
-    window[:, height + 1 : height + 2] = zero_row
-
     def prepare(n, _):
-        for tap in range(9):
-            flipped[n, :, tap * channels : (tap + 1) * channels] = weights[
-                n, (8 - tap) * channels : (9 - tap) * channels, :
-            ]
+        def tap(i, j):
+            at = (3 * i + j) * channels
+            return weights[n, at : at + channels, :]
+
+        def spot(i):
+            return slice(i * channels, (i + 1) * channels)
+
+        nothing = jnp.zeros((channels, channels), low)
+        for i in range(3):
+            for j in range(2):
+                ahead_pair[n, spot(j), spot(i)] = tap(i, j)
+                back_pair[n, spot(i), spot(j)] = tap(2 - i, 2 - j)
+        ahead_edge[n, spot(0), spot(0)] = tap(0, 2)
+        ahead_edge[n, spot(0), spot(1)] = nothing
+        ahead_edge[n, spot(1), spot(0)] = tap(1, 2)
+        ahead_edge[n, spot(1), spot(1)] = tap(2, 2)
+        back_edge[n, spot(0), spot(0)] = tap(2, 0)
+        back_edge[n, spot(1), spot(0)] = nothing
+        back_edge[n, spot(0), spot(1)] = tap(1, 0)
+        back_edge[n, spot(1), spot(1)] = tap(0, 0)
         wg_out[n] = jnp.zeros(wg_out.shape[1:], jnp.float32)
         return 0
 
@@ -187,19 +202,38 @@
 
     column = lax.rem(lax.broadcasted_iota(jnp.int32, (rows, channels), 0), width)
 
-    def patches(field):
+    area = height * width
+
+    def down(field):
+        blank = jnp.zeros((width, field.shape[1]), field.dtype)
+        lines = []
+        for at in range(0, field.shape[0], area):
+            lines += [blank, field[at : at + area - width]]
+        return jnp.concatenate(lines, axis=0)
+
+    def up(field):
+        blank = jnp.zeros((width, field.shape[1]), field.dtype)
+        lines = []
+        for at in range(0, field.shape[0], area):
+            lines += [field[at + width : at + area], blank]
+        return jnp.concatenate(lines, axis=0)
+
+    def sides(field):
         size = field.shape[0]
-        some = size // (height * width)
         place = column[:size]
         left = jnp.where(place == 0, 0.0, pltpu.roll(field, 1, 0))
         right = jnp.where(place == width - 1, 0.0, pltpu.roll(field, size - 1, 0))
-        shape = (some, height, width, channels)
-        window[:some, 1 : height + 1, :, 0:channels] = left.astype(low).reshape(shape)
-        window[:some, 1 : height + 1, :, channels : 2 * channels] = field.astype(low).reshape(shape)
-        window[:some, 1 : height + 1, :, 2 * channels : 3 * channels] = right.astype(low).reshape(shape)
-        return jnp.concatenate(
-            [window[:some, i : i + height].reshape(size, 3 * channels) for i in range(3)], axis=1
-        )
+        return left.astype(low), field.astype(low), right.astype(low)
+
+    def combine(three, pair_weights, edge_weights, contract):
+        left, middle, right = three
+        a = dot(jnp.concatenate([left, middle], axis=1), pair_weights, contract)
+        b = dot(jnp.concatenate([down(right), right], axis=1), edge_weights, contract)
+        c = channels
+        return a[:, c : 2 * c] + b[:, :c] + down(a[:, :c]) + up(a[:, 2 * c :] + b[:, c:])
+
+    def conv(n, field):
+        return combine(sides(field), ahead_pair[n], ahead_edge[n], NN)
 
     def apply_map(field, slot):
         return field + dot(field.astype(low), maps[slot].astype(low))
@@ -207,46 +241,69 @@
     def apply_flipped(field, slot):
         return field + dot(field.astype(low), maps[slot].astype(low), NT)
 
-    def advance(n, state):
-        return state + step_size * jnp.tanh(dot(patches(state), weights[n]) + biases[pl.ds(n, 1), :])
+    def split(field):
+        return tuple(field[at : at + area] for at in range(0, field.shape[0], area))
+
+    def join(fields):
+        return jnp.concatenate(fields, axis=0)
+
+    def span(i):
+        return slice(i * area, (i + 1) * area)
+
+    def advance(n, states):
+        return tuple(
+            state + step_size * jnp.tanh(conv(n, state) + biases[pl.ds(n, 1), :]) for state in states
+        )
 
     def trajectory(part, state):
-        def step(n, state):
-            states_low[n, part] = state.astype(low)
-            activation = jnp.tanh(dot(patches(state), weights[n]) + biases[pl.ds(n, 1), :])
-            slopes[n, part] = activation
-            return state + step_size * activation
-
-        return lax.fori_loop(0, blocks, step, state)
-
-    def change_of(n, part, adjoint, at=0):
-        slope = slopes[n, part, at : at + adjoint.shape[0]]
+        def step(n, states):
+            after = []
+            for i, state in enumerate(states):
+                states_low[n, part, span(i)] = state.astype(low)
+                activation = jnp.tanh(conv(n, state) + biases[pl.ds(n, 1), :])
+                slopes[n, part, span(i)] = activation
+                after.append(state + step_size * activation)
+            return tuple(after)
+
+        return join(lax.fori_loop(0, blocks, step, split(state), unroll=4))
+
+    def change_of(n, part, adjoint, i):
+        slope = slopes[n, part, span(i)]
         return step_size * (1.0 - slope * slope) * adjoint
 
     def retreat(part, adjoint):
-        def step(i, adjoint):
+        def step(i, adjoints):
             n = blocks - 1 - i
-            return adjoint + dot(patches(change_of(n, part, adjoint)), flipped[n], NT)
-
-        return lax.fori_loop(0, blocks, step, adjoint)
+            return tuple(
+                adjoint + combine(sides(change_of(n, part, adjoint, at)), back_pair[n], back_edge[n], NT)
+                for at, adjoint in enumerate(adjoints)
+            )
+
+        return join(lax.fori_loop(0, blocks, step, split(adjoint), unroll=4))
 
     divisor = 1.0 / images_all
 
-    def sweep(part, adjoint, at=0):
-        def step(i, adjoint):
+    def sweep(part, adjoint, first=0):
+        def step(i, adjoints):
             n = blocks - 1 - i
-            change = change_of(n, part, adjoint, at)
-            bg_out[pl.ds(n, 1), :] += jnp.sum(change, axis=0, keepdims=True) * divisor
-            spots = patches(change)
-            adjoint = adjoint + dot(spots, flipped[n], NT)
-            grads = dot(states_low[n, part, at : at + adjoint.shape[0]], spots, TN) * divisor
+            after = []
+            spots = []
+            for at, adjoint in enumerate(adjoints):
+                change = change_of(n, part, adjoint, first + at)
+                bg_out[pl.ds(n, 1), :] += jnp.sum(change, axis=0, keepdims=True) * divisor
+                three = sides(change)
+                after.append(adjoint + combine(three, back_pair[n], back_edge[n], NT))
+                line = jnp.concatenate(three, axis=1)
+                spots.append(jnp.concatenate([down(line), line, up(line)], axis=1))
+            used = states_low[n, part, first * area : (first + len(spots)) * area]
+            grads = dot(used, join(spots), TN) * divisor
             for tap in range(9):
                 wg_out[n, (8 - tap) * channels : (9 - tap) * channels, :] += grads[
                     :, tap * channels : (tap + 1) * channels
                 ]
-            return adjoint
-
-        return lax.fori_loop(0, blocks, step, adjoint)
+            return tuple(after)
+
+        return join(lax.fori_loop(0, blocks, step, split(adjoint), unroll=4))
 
     def rows_of(slot):
         return pl.ds(pl.multiple_of(slot * share, share), share)
@@ -362,7 +419,7 @@
         map_copy(before, me).wait_recv()
 
     starts = jnp.where(me == 0, start_image, apply_map(start_image, jnp.where(me == 0, me, before)))
-    relaxed = lax.fori_loop(0, blocks, advance, starts)
+    relaxed = join(lax.fori_loop(0, blocks, advance, split(starts), unroll=4))
     chain_start(0, relaxed - apply_map(start_image, me))
 
     same_side(hand_on)
@@ -406,7 +463,7 @@
         part = nth_other(parts - 2)
         for i in range(count):
             line_round(1, parts - 1, (i,))
-            sweep(part, adj_all[part, i * piece : (i + 1) * piece], i * piece)
+            sweep(part, adj_all[part, i * piece : (i + 1) * piece], i)
 
     def map_sent(to):
         if pair == 1:
@@ -477,8 +534,10 @@
             pltpu.VMEM((blocks, channels), f32),
             pltpu.VMEM((rows, channels), f32),
             dma((4,)),
-            pltpu.VMEM((blocks, channels, 9 * channels), low),
-            pltpu.VMEM((count, height + 2, width, 3 * channels), low),
+            pltpu.VMEM((blocks, 2 * channels, 3 * channels), low),
+            pltpu.VMEM((blocks, 2 * channels, 2 * channels), low),
+            pltpu.VMEM((blocks, 3 * channels, 2 * channels), low),
+            pltpu.VMEM((blocks, 2 * channels, 2 * channels), low),
             pltpu.VMEM((groups, channels, channels), f32),
             pltpu.VMEM((blocks, parts, rows, channels), low),
             pltpu.VMEM((blocks, parts, rows, channels), f32),

time: 59.5 us -> 57.7 us (0.970)
  Pallas kernels: 55.9 us -> 54.1 us
    pallas_call x1, Pallas kernels: 55.9 us -> 54.1 us  [shards(): pl.pallas_call(functools.partial(kernel, dims), out_shape=(pltpu.VMEM((2,...]
where the time goes in v1:
time: 57.7 us; the launch traced here: 57.6 us
  Pallas kernels  54.1 us (94%)
  local copies, waits for them, and re-layouts  2.81 us (5%)
  between operations  0.64 us (1%)
    pallas_call x1, Pallas kernels, shards(): pl.pallas_call(functools.partial(kernel, dims), out_shape=(pltpu.VMEM((2,...  54.1 us
    unnamed x2, local copies, waits for them, and re-layouts  1.99 us

profile of v1, /device:TPU:0, one launch (start us, length us, event | category | flops | bytes accessed | tf_op | source)
XLA Modules:
  0.0 57.6 jit_solution(6297771617223835901)
XLA Ops:
  0.6 54.1 %shard_map.75 = (f32[2,512,128]{2,1,0:T(8,128)S(1)}, f32[4,1152,128]{2,1,0:T(8,128)S(1)}, f32[4,128]{1,0:T(4,128)S(1)}) custom-call(f32[512,128]{1,0:T(8,128)} %bitcast.8, bf16[4,1152,128]{2,1,0:T(8,128)(2,1)} %bitcast.7, f32[4,128]{1,0:T(4,128)} %biases_in.1, f32[512,128]{1,0:T(8,128)} %bitcast.9), custom_call_target="tpu_custom_call" | custom-call | tf_op jit(solution)/shard_map/pallas_call | solution.py:522
  54.8 1.4 %copy.10 = f32[4,3,3,128,128]{4,3,2,1,0:T(8,128)} copy(f32[4,3,3,128,128]{4,3,2,1,0:T(8,128)S(1)} %bitcast.6) | data formatting | bytes 4718592
  56.2 0.8 %fusion = (f32[1,512,128]{2,1,0:T(8,128)}, f32[1,512,128]{2,1,0:T(8,128)}) fusion(f32[2,512,128]{2,1,0:T(8,128)S(1)} %get-tuple-element.7), kind=kLoop, calls=%fused_computation | loop fusion | bytes 1048576 | tf_op jit(solution)/shard_map/slice | solution.py:571
  57.0 0.6 %copy.11 = f32[4,128]{1,0:T(4,128)} copy(f32[4,128]{1,0:T(4,128)S(1)} %get-tuple-element.15) | data formatting | bytes 4096

commit v2 on v1

--- a/solution.py
+++ b/solution.py
@@ -30,7 +30,6 @@
     both_out,
     wg_out,
     bg_out,
-    images,
     weights,
     biases,
     end_grad,
@@ -58,6 +57,17 @@
     right_send,
     left_send,
     line_recv,
+    part_images,
+    other_starts,
+    other_fine,
+    handoff,
+    pass_send,
+    pass_recv,
+    part_grads,
+    share_send,
+    share_recv,
+    spread_send,
+    spread_recv,
 ):
     groups, parts, count, height, width, images_all = dims
     rows, channels = images_in.shape
@@ -78,7 +88,7 @@
     loads = [
         pltpu.make_async_copy(source, target, load_sems.at[i])
         for i, (source, target) in enumerate(
-            ((weights_in, weights), (images_in, images), (biases_in, biases), (end_grad_in, end_grad))
+            ((weights_in, weights), (images_in, part_images.at[z]), (biases_in, biases), (end_grad_in, end_grad))
         )
     ]
     for load in loads:
@@ -86,13 +96,10 @@
     barrier = pltpu.get_barrier_semaphore()
     others(lambda ahead, to: pl.semaphore_signal(barrier, inc=1, device_id={"layer": to}, device_id_type=MESH))
 
-    @pl.when(not_first)
-    def _():
-        pl.semaphore_signal(barrier, inc=1, device_id={"dp": z - 1}, device_id_type=MESH)
-
-    @pl.when(not_last)
-    def _():
-        pl.semaphore_signal(barrier, inc=1, device_id={"dp": z + 1}, device_id_type=MESH)
+    for ahead in range(1, parts):
+        pl.semaphore_signal(
+            barrier, inc=1, device_id={"dp": lax.rem(z + ahead, parts)}, device_id_type=MESH
+        )
 
     loads[0].wait()
     centre = slice(4 * channels, 5 * channels)
@@ -101,8 +108,7 @@
         total = total + weights[n, centre, :].astype(jnp.float32)
     maps[me] = step_size * total
 
-    neighbours = jnp.where(not_first, 1, 0) + jnp.where(not_last, 1, 0)
-    pl.semaphore_wait(barrier, groups - 1 + neighbours)
+    pl.semaphore_wait(barrier, groups - 1 + parts - 1)
 
     def map_copy(slot, to):
         return pltpu.make_async_remote_copy(
@@ -172,6 +178,105 @@
 
     for load in loads[1:]:
         load.wait()
+
+    lead = lax.rem(me, 2) == 0
+
+    def rows_of(slot):
+        return pl.ds(pl.multiple_of(slot * share, share), share)
+
+    def other_planes(body, who=True):
+        for away in range(1, parts):
+
+            @pl.when(who & (z + away < parts))
+            def _():
+                body(z + away)
+
+            @pl.when(who & (z - away >= 0))
+            def _():
+                body(z - away)
+
+    def share_copy(part, to):
+        return pltpu.make_async_remote_copy(
+            src_ref=end_grad.at[rows_of(me)],
+            dst_ref=part_grads.at[part, rows_of(me)],
+            send_sem=share_send.at[to],
+            recv_sem=share_recv.at[part],
+            device_id={"dp": to},
+            device_id_type=MESH,
+        )
+
+    def spread_copy(part, source, to):
+        return pltpu.make_async_remote_copy(
+            src_ref=part_grads.at[part, rows_of(source)],
+            dst_ref=part_grads.at[part, rows_of(source)],
+            send_sem=spread_send.at[part, to // 2],
+            recv_sem=spread_recv.at[part, source],
+            device_id={"layer": to},
+            device_id_type=MESH,
+        )
+
+    def odd_others(body):
+        def step(i, _):
+            to = 2 * i + 1
+
+            @pl.when(to != me)
+            def _():
+                body(to)
+
+            return 0
+
+        lax.fori_loop(0, groups // 2, step, 0)
+
+    other_planes(lambda to: share_copy(z, to).start(), me >= 0)
+
+    line = (states_all, adj_all, part_images)
+    piece = rows // count
+
+    def line_copy(which, block, part, to, sends):
+        where = line[which].at[block, part * piece : (part + 1) * piece]
+        return pltpu.make_async_remote_copy(
+            src_ref=where,
+            dst_ref=where,
+            send_sem=sends.at[which, block, part],
+            recv_sem=line_recv.at[which, block, part],
+            device_id={"dp": to},
+            device_id_type=MESH,
+        )
+
+    def go_right(which, block, part):
+        @pl.when(not_last)
+        def _():
+            line_copy(which, block, part, z + 1, right_send).start()
+
+    def go_left(which, block, part):
+        @pl.when(not_first)
+        def _():
+            line_copy(which, block, part, z - 1, left_send).start()
+
+    def takes(which):
+        return jnp.logical_not(lead) if which == 1 else lead
+
+    def line_start(which):
+        @pl.when(takes(which))
+        def _():
+            for part in range(count):
+                go_right(which, z, part)
+                go_left(which, z, part)
+
+    def line_round(which, away, pieces=range(count)):
+        for part in pieces:
+
+            @pl.when(takes(which) & (z - away >= 0))
+            def _():
+                line_copy(which, z - away, part, z, right_send).wait_recv()
+                go_right(which, z - away, part)
+
+            @pl.when(takes(which) & (z + away < parts))
+            def _():
+                line_copy(which, z + away, part, z, left_send).wait_recv()
+                go_left(which, z + away, part)
+
+    line_start(2)
 
     def prepare(n, _):
         def tap(i, j):
@@ -305,9 +410,6 @@
 
         return join(lax.fori_loop(0, blocks, step, split(adjoint), unroll=4))
 
-    def rows_of(slot):
-        return pl.ds(pl.multiple_of(slot * share, share), share)
-
     def out_copy(phase, source, to):
         return pltpu.make_async_remote_copy(
             src_ref=residue.at[phase, rows_of(to)],
@@ -356,71 +458,88 @@
         others(lambda ahead, to: back_copy(phase, to, me).wait_recv())
         return error[phase]
 
-    line = (states_all, adj_all)
-
-    piece = rows // count
-
-    def line_copy(which, block, part, to, sends):
-        where = line[which].at[block, part * piece : (part + 1) * piece]
-        return pltpu.make_async_remote_copy(
-            src_ref=where,
-            dst_ref=where,
-            send_sem=sends.at[which, block, part],
-            recv_sem=line_recv.at[which, block, part],
-            device_id={"dp": to},
-            device_id_type=MESH,
-        )
-
-    def go_right(which, block, part):
-        @pl.when(not_last)
-        def _():
-            line_copy(which, block, part, z + 1, right_send).start()
-
-    def go_left(which, block, part):
-        @pl.when(not_first)
-        def _():
-            line_copy(which, block, part, z - 1, left_send).start()
-
-    def line_start(which):
-        for part in range(count):
-            go_right(which, z, part)
-            go_left(which, z, part)
-
-    def line_round(which, away, pieces=range(count)):
-        for part in pieces:
-
-            @pl.when(z - away >= 0)
-            def _():
-                line_copy(which, z - away, part, z, right_send).wait_recv()
-                go_right(which, z - away, part)
-
-            @pl.when(z + away < parts)
-            def _():
-                line_copy(which, z + away, part, z, left_send).wait_recv()
-                go_left(which, z + away, part)
 
     def nth_other(i):
         back_side = parts - 1 - z
         paired = jnp.where(z < back_side, z, back_side)
         near = i // 2 + 1
-        near_part = jnp.where(i % 2 == 0, z - near, z + near)
+        outward = jnp.where(z > back_side, near, -near)
+        near_part = jnp.where(i % 2 == 0, z + outward, z - outward)
         far = i - paired + 1
         far_part = jnp.where(z > back_side, z - far, z + far)
         return jnp.where(i < 2 * paired, near_part, far_part)
 
+    def start_of(field):
+        return jnp.where(me == 0, field, apply_map(field, jnp.where(me == 0, me, before)))
+
+    def relax(start):
+        return join(lax.fori_loop(0, blocks, advance, split(start), unroll=4))
+
+    def relax_other(i):
+        @pl.when(lead)
+        def _():
+            part = nth_other(i)
+            start = start_of(part_images[part])
+            other_starts[part] = start
+            other_fine[part] = relax(start)
+
+    def share_on(i):
+        part = nth_other(i)
+        share_copy(part, z).wait_recv()
+        odd_others(lambda to: spread_copy(part, me, to).start())
+
+    def retreat_other(i):
+        @pl.when(jnp.logical_not(lead))
+        def _():
+            part = nth_other(i)
+            others(lambda ahead, source: spread_copy(part, source, me).wait_recv())
+            ends = ends_of(part_grads[part])
+            other_starts[part] = ends
+            other_fine[part] = retreat(part, ends)
+
+    def pass_copy(which, part, i):
+        where = pl.ds(i * piece, piece)
+        return pltpu.make_async_remote_copy(
+            src_ref=handoff.at[part, where],
+            dst_ref=line[which].at[part, where],
+            send_sem=pass_send.at[part, i],
+            recv_sem=pass_recv.at[which, part, i],
+            device_id={"layer": partner},
+            device_id_type=MESH,
+        )
+
+    def pass_on(which, i, pieces=range(count)):
+        part = nth_other(i)
+        apply = apply_map if which == 0 else apply_flipped
+
+        @pl.when(takes(which))
+        def _():
+            for at in pieces:
+                where = slice(at * piece, (at + 1) * piece)
+                change = line[which][part, where] - other_starts[part, where]
+                handoff[part, where] = apply(change, me) + other_fine[part, where]
+                pass_copy(which, part, at).start()
+
+    def pass_wait(which, i, pieces=range(count)):
+        part = nth_other(i)
+
+        @pl.when(jnp.logical_not(takes(which)))
+        def _():
+            for at in pieces:
+                pass_copy(which, part, at).wait_recv()
+
     def other_trajectory(i):
         part = nth_other(i)
         trajectory(part, states_all[part])
 
-    start_image = images[...]
+    start_image = part_images[z]
 
     @pl.when(me != 0)
     def _():
         map_copy(before, me).wait_recv()
 
-    starts = jnp.where(me == 0, start_image, apply_map(start_image, jnp.where(me == 0, me, before)))
-    relaxed = join(lax.fori_loop(0, blocks, advance, split(starts), unroll=4))
-    chain_start(0, relaxed - apply_map(start_image, me))
+    starts = start_of(start_image)
+    chain_start(0, relax(starts) - apply_map(start_image, me))
 
     same_side(hand_on)
 
@@ -431,38 +550,76 @@
 
     if pair == 2:
         others(wait_map)
+    def ends_of(field):
+        return jnp.where(me == last, field, apply_flipped(field, after))
+
     end = end_grad[...]
-    ends_adj = jnp.where(me == last, end, apply_flipped(end, after))
+    ends_adj = ends_of(end)
     back = apply_flipped(end, me)
+    others_count = parts - 1
+
+    def images_on(i):
+        if i < others_count:
+            line_round(2, i + 1)
+
+    def relax_on(i):
+        if i < others_count:
+            relax_other(i)
+
+    def states_on(i):
+        if i < others_count:
+            line_round(0, i + 1)
+            pass_on(0, i)
+
+    def follow(i):
+        if i < others_count:
+            pass_wait(0, i)
+            other_trajectory(i)
+            retreat_other(i)
+
     chain_scan(0)
+    for i in range(others_count):
+        share_on(i)
+    images_on(0)
+    relax_on(0)
     corrected = starts + chain_finish(0)
     states_all[z] = corrected
     line_start(0)
     both_out[0] = trajectory(z, corrected)
 
     chain_start(1, retreat(z, ends_adj) - back)
-    if parts > 1:
-        line_round(0, 1)
-        other_trajectory(0)
+    images_on(1)
+    relax_on(1)
+    states_on(0)
+    follow(0)
     chain_scan(1)
-    if parts > 2:
-        line_round(0, 2)
-        other_trajectory(1)
+    images_on(2)
+    relax_on(2)
+    states_on(1)
+    follow(1)
     adjoint = ends_adj + chain_finish(1)
     adj_all[z] = adjoint
     line_start(1)
+    for i in range(2, others_count):
+        if i > 2:
+            images_on(i)
+            relax_on(i)
+        states_on(i)
     both_out[1] = sweep(z, adjoint)
-    for i in range(2, parts - 1):
-        line_round(0, i + 1)
-        other_trajectory(i)
-    for i in range(parts - 2):
+    for i in range(2, others_count):
+        follow(i)
+    for i in range(others_count - 1):
         line_round(1, i + 1)
+        pass_on(1, i)
+        pass_wait(1, i)
         part = nth_other(i)
         sweep(part, adj_all[part])
     if parts > 1:
         part = nth_other(parts - 2)
         for i in range(count):
             line_round(1, parts - 1, (i,))
+            pass_on(1, parts - 2, (i,))
+            pass_wait(1, parts - 2, (i,))
             sweep(part, adj_all[part, i * piece : (i + 1) * piece], i)
 
     def map_sent(to):
@@ -494,18 +651,32 @@
             back_copy(phase, me, to).wait_send()
 
     others(sent)
-    for which in range(2):
+    for which in range(3):
         for away in range(parts):
 
-            @pl.when((z - away >= 0) & not_last)
+            @pl.when(takes(which) & (z - away >= 0) & not_last)
             def _():
                 for part in range(count):
                     line_copy(which, z - away, part, z + 1, right_send).wait_send()
 
-            @pl.when((z + away < parts) & not_first)
+            @pl.when(takes(which) & (z + away < parts) & not_first)
             def _():
                 for part in range(count):
                     line_copy(which, z + away, part, z - 1, left_send).wait_send()
+
+    other_planes(lambda to: share_copy(z, to).wait_send(), me >= 0)
+
+    def passed(part):
+        for i in range(count):
+            for which in range(2):
+
+                @pl.when(takes(which))
+                def _():
+                    pass_copy(which, part, i).wait_send()
+
+        odd_others(lambda to: spread_copy(part, me, to).wait_send())
+
+    other_planes(passed, me >= 0)
 
 
 def shards(images, weights, biases, end_grad):
@@ -529,7 +700,6 @@
         in_specs=[pl.BlockSpec(memory_space=pltpu.HBM)] * 4,
         out_specs=(vmem,) * 3,
         scratch_shapes=[
-            pltpu.VMEM((rows, channels), f32),
             pltpu.VMEM((blocks, 9 * channels, channels), low),
             pltpu.VMEM((blocks, channels), f32),
             pltpu.VMEM((rows, channels), f32),
@@ -554,9 +724,20 @@
             dma((2, groups)),
             dma((2, groups)),
             dma((2, groups)),
+            dma((3, parts, count)),
+            dma((3, parts, count)),
+            dma((3, parts, count)),
+            pltpu.VMEM((parts, rows, channels), f32),
+            pltpu.VMEM((parts, rows, channels), f32),
+            pltpu.VMEM((parts, rows, channels), f32),
+            pltpu.VMEM((parts, rows, channels), f32),
+            dma((parts, count)),
             dma((2, parts, count)),
-            dma((2, parts, count)),
-            dma((2, parts, count)),
+            pltpu.VMEM((parts, rows, channels), f32),
+            dma((parts,)),
+            dma((parts,)),
+            dma((parts, groups // 2)),
+            dma((parts, groups)),
         ],
         compiler_params=pltpu.CompilerParams(
             collective_id=0, has_side_effects=True, vmem_limit_bytes=61 << 20

time: 57.7 us -> 53.8 us (0.932)
  Pallas kernels: 54.1 us -> 50.2 us
    pallas_call x1, Pallas kernels: 54.1 us -> 50.2 us  [shards(): pl.pallas_call(functools.partial(kernel, dims), out_shape=(pltpu.VMEM((2,...]
where the time goes in v2:
time: 53.8 us; the launch traced here: 53.6 us
  Pallas kernels  50.2 us (93%)
  local copies, waits for them, and re-layouts  2.81 us (5%)
  between operations  0.64 us (1%)
    pallas_call x1, Pallas kernels, shards(): pl.pallas_call(functools.partial(kernel, dims), out_shape=(pltpu.VMEM((2,...  50.2 us
    unnamed x2, local copies, waits for them, and re-layouts  1.99 us

profile of v2, /device:TPU:0, one launch (start us, length us, event | category | flops | bytes accessed | tf_op | source)
XLA Modules:
  0.0 53.6 jit_solution(2852508215363524116)
XLA Ops:
  0.6 50.2 %shard_map.75 = (f32[2,512,128]{2,1,0:T(8,128)S(1)}, f32[4,1152,128]{2,1,0:T(8,128)S(1)}, f32[4,128]{1,0:T(4,128)S(1)}) custom-call(f32[512,128]{1,0:T(8,128)} %bitcast.8, bf16[4,1152,128]{2,1,0:T(8,128)(2,1)} %bitcast.7, f32[4,128]{1,0:T(4,128)} %biases_in.1, f32[512,128]{1,0:T(8,128)} %bitcast.9), custom_call_target="tpu_custom_call" | custom-call | tf_op jit(solution)/shard_map/pallas_call | solution.py:693
  50.8 1.4 %copy.10 = f32[4,3,3,128,128]{4,3,2,1,0:T(8,128)} copy(f32[4,3,3,128,128]{4,3,2,1,0:T(8,128)S(1)} %bitcast.6) | data formatting | bytes 4718592
  52.2 0.8 %fusion = (f32[1,512,128]{2,1,0:T(8,128)}, f32[1,512,128]{2,1,0:T(8,128)}) fusion(f32[2,512,128]{2,1,0:T(8,128)S(1)} %get-tuple-element.7), kind=kLoop, calls=%fused_computation | loop fusion | bytes 1048576 | tf_op jit(solution)/shard_map/slice | solution.py:752
  53.0 0.6 %copy.11 = f32[4,128]{1,0:T(4,128)} copy(f32[4,128]{1,0:T(4,128)S(1)} %get-tuple-element.15) | data formatting | bytes 4096

commit v3 on v2

--- a/solution.py
+++ b/solution.py
@@ -575,6 +575,9 @@
         if i < others_count:
             pass_wait(0, i)
             other_trajectory(i)
+
+    def answer(i):
+        if i < others_count:
             retreat_other(i)
 
     chain_scan(0)
@@ -593,10 +596,12 @@
     states_on(0)
     follow(0)
     chain_scan(1)
+    answer(0)
     images_on(2)
     relax_on(2)
     states_on(1)
     follow(1)
+    answer(1)
     adjoint = ends_adj + chain_finish(1)
     adj_all[z] = adjoint
     line_start(1)
@@ -608,19 +613,26 @@
     both_out[1] = sweep(z, adjoint)
     for i in range(2, others_count):
         follow(i)
-    for i in range(others_count - 1):
-        line_round(1, i + 1)
-        pass_on(1, i)
-        pass_wait(1, i)
-        part = nth_other(i)
-        sweep(part, adj_all[part])
+    early = range(count // 2)
+    late = range(count // 2, count)
     if parts > 1:
-        part = nth_other(parts - 2)
-        for i in range(count):
-            line_round(1, parts - 1, (i,))
-            pass_on(1, parts - 2, (i,))
-            pass_wait(1, parts - 2, (i,))
-            sweep(part, adj_all[part, i * piece : (i + 1) * piece], i)
+        line_round(1, 1, early)
+    for i in range(2, others_count):
+        answer(i)
+    for i in range(others_count):
+        pass_on(1, i, early)
+        line_round(1, i + 1, late)
+        pass_on(1, i, late)
+        if i < others_count - 1:
+            pass_wait(1, i)
+            part = nth_other(i)
+            sweep(part, adj_all[part])
+            line_round(1, i + 2, early)
+        else:
+            part = nth_other(i)
+            for at in range(count):
+                pass_wait(1, i, (at,))
+                sweep(part, adj_all[part, at * piece : (at + 1) * piece], at)
 
     def map_sent(to):
         if pair == 1:
@@ -677,6 +689,19 @@
         odd_others(lambda to: spread_copy(part, me, to).wait_send())
 
     other_planes(passed, me >= 0)
+
+
+def write_out(both, wg, bg, ends_out, starts_out, wg_out, bg_out, sems):
+    copies = [
+        pltpu.make_async_copy(source, target, sems.at[i])
+        for i, (source, target) in enumerate(
+            ((wg, wg_out), (both.at[0], ends_out), (both.at[1], starts_out), (bg, bg_out))
+        )
+    ]
+    for copy in copies:
+        copy.start()
+    for copy in copies:
+        copy.wait()
 
 
 def shards(images, weights, biases, end_grad):
@@ -749,7 +774,21 @@
         end_grad.reshape(rows, channels),
     )
     shape = (1,) + images.shape
-    return (both[0].reshape(shape), both[1].reshape(shape), wg.reshape(weights.shape), bg)
+    hbm = pl.BlockSpec(memory_space=pltpu.HBM)
+    ends, starts, wg, bg = pl.pallas_call(
+        write_out,
+        out_shape=(
+            jax.ShapeDtypeStruct((rows, channels), f32),
+            jax.ShapeDtypeStruct((rows, channels), f32),
+            jax.ShapeDtypeStruct((blocks, 9 * channels, channels), f32),
+            jax.ShapeDtypeStruct((blocks, channels), f32),
+        ),
+        in_specs=[vmem] * 3,
+        out_specs=(hbm,) * 4,
+        scratch_shapes=[dma((4,))],
+        compiler_params=pltpu.CompilerParams(vmem_limit_bytes=1 << 20),
+    )(*(pltpu.with_memory_space_constraint(x, pltpu.VMEM) for x in (both, wg, bg)))
+    return (ends.reshape(shape), starts.reshape(shape), wg.reshape(weights.shape), bg)
 
 
 def solution(mesh):

time: 53.8 us -> 51.4 us (0.955)
  local copies, waits for them, and re-layouts: 2.81 us -> 0 us
    unnamed x2 -> x0, local copies, waits for them, and re-layouts: 1.99 us -> none
    pallas_call x0 -> x1, Pallas kernels: none -> 1.6 us  [shards(): pl.pallas_call(write_out, out_shape=(jax.ShapeDtypeStruct((rows, channels...]
    pallas_call x1, Pallas kernels: 50.2 us -> 48.9 us  [shards(): pl.pallas_call(functools.partial(kernel, dims), out_shape=(pltpu.VMEM((2,...]
    slice x1 -> x0, local copies, waits for them, and re-layouts: 0.82 us -> none  [shards(): both[1].reshape(shape)]
where the time goes in v3:
time: 51.4 us; the launch traced here: 51.3 us
  Pallas kernels  50.5 us (98%)
  between operations  0.8 us (2%)
    pallas_call x1, Pallas kernels, shards(): pl.pallas_call(functools.partial(kernel, dims), out_shape=(pltpu.VMEM((2,...  48.9 us
    pallas_call x1, Pallas kernels, shards(): pl.pallas_call(write_out, out_shape=(jax.ShapeDtypeStruct((rows, channels...  1.6 us

profile of v3, /device:TPU:0, one launch (start us, length us, event | category | flops | bytes accessed | tf_op | source)
XLA Modules:
  0.0 51.3 jit_solution(14085819056876232970)
XLA Ops:
  0.6 48.9 %shard_map.75 = (f32[2,512,128]{2,1,0:T(8,128)S(1)}, f32[4,1152,128]{2,1,0:T(8,128)S(1)}, f32[4,128]{1,0:T(4,128)S(1)}) custom-call(f32[512,128]{1,0:T(8,128)} %bitcast.7, bf16[4,1152,128]{2,1,0:T(8,128)(2,1)} %bitcast.6, f32[4,128]{1,0:T(4,128)} %biases_in.1, f32[512,128]{1,0:T(8,128)} %bitcast.8), custom_call_target="tpu_custom_call" | custom-call | tf_op jit(solution)/shard_map/pallas_call | solution.py:718
  49.5 1.6 %shard_map.76 = (f32[512,128]{1,0:T(8,128)}, f32[512,128]{1,0:T(8,128)}, f32[4,1152,128]{2,1,0:T(8,128)}, f32[4,128]{1,0:T(4,128)}) custom-call(f32[2,512,128]{2,1,0:T(8,128)S(1)} %get-tuple-element.11.both, f32[4,1152,128]{2,1,0:T(8,128)S(1)} %get-tuple-element.12.wg, f32[4,128]{1,0:T(4,128)S(1)} %get-tuple-element.13.bg), custom_call_target="tpu_custom_call" | custom-call | tf_op jit(solution)/shard_map/pallas_call | solution.py:778

commit v4 on v3

--- a/solution.py
+++ b/solution.py
@@ -68,6 +68,7 @@
     share_recv,
     spread_send,
     spread_recv,
+    pair_maps,
 ):
     groups, parts, count, height, width, images_all = dims
     rows, channels = images_in.shape
@@ -121,36 +122,32 @@
         )
 
     last = groups - 1
-    after = lax.rem(me + 1, groups)
-    before = lax.rem(me + last, groups)
-    pair = 2 if groups % 2 == 0 else 1
-    partner = me + 1 - 2 * lax.rem(me, 2) if pair == 2 else me
+    after = jnp.minimum(me + 1, last)
+    before = jnp.maximum(me - 1, 0)
+    partner = me + 1 - 2 * lax.rem(me, 2)
+    inner = (me > 0) & (me < last)
 
     def same_side(body):
         def step(ahead, _):
-            body(lax.rem(me + pair * ahead, groups))
+            body(lax.rem(me + 2 * ahead, groups))
             return 0
 
-        lax.fori_loop(1, groups // pair, step, 0)
-
-    map_copy(me, after).start()
-    if pair == 2:
-
-        @pl.when(partner != after)
-        def _():
-            map_copy(me, partner).start()
-
-    def send_map(to):
-        if pair == 1:
-
-            @pl.when(to != after)
-            def _():
-                map_copy(me, to).start()
-
-        else:
-            map_copy(me, to).start()
-
-    same_side(send_map)
+        lax.fori_loop(1, groups // 2, step, 0)
+
+    def map_sends(body):
+        @pl.when(me < last)
+        def _():
+            body(after)
+
+        @pl.when(lax.rem(me, 2) == 1)
+        def _():
+            body(partner)
+
+        @pl.when(inner)
+        def _():
+            same_side(body)
+
+    map_sends(lambda to: map_copy(me, to).start())
 
     def hand_copy(slot):
         return pltpu.make_async_remote_copy(
@@ -163,18 +160,16 @@
         )
 
     def is_handed(slot):
-        return lax.rem(slot + 1, groups) != partner
+        return (slot > 0) & (slot < last) & (slot + 1 != partner)
 
     def hand_on(slot):
-        @pl.when((slot != before) | (me == 0))
+        @pl.when((slot > 0) & (slot < last))
         def _():
             map_copy(slot, me).wait_recv()
 
-        if pair == 2:
-
-            @pl.when(is_handed(slot))
-            def _():
-                hand_copy(slot).start()
+        @pl.when(is_handed(slot))
+        def _():
+            hand_copy(slot).start()
 
     for load in loads[1:]:
         load.wait()
@@ -340,11 +335,11 @@
     def conv(n, field):
         return combine(sides(field), ahead_pair[n], ahead_edge[n], NN)
 
-    def apply_map(field, slot):
-        return field + dot(field.astype(low), maps[slot].astype(low))
-
-    def apply_flipped(field, slot):
-        return field + dot(field.astype(low), maps[slot].astype(low), NT)
+    def apply_map(field, slot, table=maps):
+        return field + dot(field.astype(low), table[slot].astype(low))
+
+    def apply_flipped(field, slot, table=maps):
+        return field + dot(field.astype(low), table[slot].astype(low), NT)
 
     def split(field):
         return tuple(field[at : at + area] for at in range(0, field.shape[0], area))
@@ -430,34 +425,75 @@
             device_id_type=MESH,
         )
 
+    pairs = groups // 2
+    ends = (0, last)
+
     def chain_start(phase, value):
         residue[phase] = value
-        others(lambda ahead, to: out_copy(phase, me, to).start())
+
+        @pl.when(me != ends[1 - phase])
+        def _():
+            others(lambda ahead, to: out_copy(phase, me, to).start())
+
         gathered[phase, me] = residue[phase, rows_of(me)]
 
+    def pair_up(m, _):
+        one = maps[2 * m]
+        two = maps[2 * m + 1]
+        pair_maps[m] = one + two + dot(one.astype(low), two.astype(low))
+        return 0
+
     def chain_scan(phase):
+        apply = apply_map if phase == 0 else apply_flipped
+
+        def deliver(k, value):
+            @pl.when(k != me)
+            def _():
+                spread[phase, k] = value
+                back_copy(phase, me, k).start()
+
+            @pl.when(k == me)
+            def _():
+                error[phase, rows_of(me)] = value
+
+        def arrived(k):
+            @pl.when(k != me)
+            def _():
+                out_copy(phase, k, me).wait_recv()
+
+        def pair_of(i):
+            m = i if phase == 0 else pairs - 1 - i
+            return 2 * m + phase, 2 * m + 1 - phase, m
+
         def step(i, carried):
-            k = i if phase == 0 else groups - 1 - i
-
-            @pl.when(k != me)
-            def _():
-                spread[phase, k] = carried
-                back_copy(phase, me, k).start()
-                out_copy(phase, k, me).wait_recv()
-
-            @pl.when(k == me)
-            def _():
-                error[phase, rows_of(me)] = carried
-
-            mapped = apply_map(carried, k) if phase == 0 else apply_flipped(carried, k)
-            return mapped + gathered[phase, k]
-
-        lax.fori_loop(0, groups, step, jnp.zeros((share, channels), jnp.float32))
+            one, two, m = pair_of(i)
+            deliver(one, carried)
+            moved = apply(carried, one)
+            jumped = apply(carried, m, pair_maps)
+            arrived(one)
+            deliver(two, moved + gathered[phase, one])
+            jumped = jumped + apply(gathered[phase, one], two)
+            arrived(two)
+            return jumped + gathered[phase, two]
+
+        one, two, _ = pair_of(0)
+        arrived(one)
+        deliver(two, gathered[phase, one])
+        carried = apply(gathered[phase, one], two)
+        arrived(two)
+        carried = lax.fori_loop(1, pairs - 1, step, carried + gathered[phase, two])
+        one, two, _ = pair_of(pairs - 1)
+        deliver(one, carried)
+        moved = apply(carried, one)
+        arrived(one)
+        deliver(two, moved + gathered[phase, one])
 
     def chain_finish(phase):
-        others(lambda ahead, to: back_copy(phase, to, me).wait_recv())
-        return error[phase]
-
+        @pl.when(me != ends[phase])
+        def _():
+            others(lambda ahead, to: back_copy(phase, to, me).wait_recv())
+
+        return jnp.where(me == ends[phase], 0.0, error[phase])
 
     def nth_other(i):
         back_side = parts - 1 - z
@@ -493,9 +529,9 @@
         def _():
             part = nth_other(i)
             others(lambda ahead, source: spread_copy(part, source, me).wait_recv())
-            ends = ends_of(part_grads[part])
-            other_starts[part] = ends
-            other_fine[part] = retreat(part, ends)
+            cotangent = ends_of(part_grads[part])
+            other_starts[part] = cotangent
+            other_fine[part] = retreat(part, cotangent)
 
     def pass_copy(which, part, i):
         where = pl.ds(i * piece, piece)
@@ -544,12 +580,16 @@
     same_side(hand_on)
 
     def wait_map(ahead, source):
-        @pl.when((lax.rem(source - me + groups, pair) != 0) & ((source != before) | (me == 0)))
+        across = lax.rem(source - me + groups, 2) != 0
+        sent = (source > 0) & ((source < last) | (me == last - 1))
+
+        @pl.when(across & sent & (source != me - 1))
         def _():
             map_copy(source, me).wait_recv()
 
-    if pair == 2:
-        others(wait_map)
+    others(wait_map)
+    lax.fori_loop(1, pairs - 1, pair_up, 0)
+
     def ends_of(field):
         return jnp.where(me == last, field, apply_flipped(field, after))
 
@@ -634,33 +674,25 @@
                 pass_wait(1, i, (at,))
                 sweep(part, adj_all[part, at * piece : (at + 1) * piece], at)
 
-    def map_sent(to):
-        if pair == 1:
-
-            @pl.when(to != after)
-            def _():
-                map_copy(me, to).wait_send()
-
-        else:
-            map_copy(me, to).wait_send()
-
-            @pl.when(is_handed(to))
-            def _():
-                hand_copy(to).wait_send()
-
-    map_copy(me, after).wait_send()
-    if pair == 2:
-
-        @pl.when(partner != after)
-        def _():
-            map_copy(me, partner).wait_send()
-
-    same_side(map_sent)
+    map_sends(lambda to: map_copy(me, to).wait_send())
+
+    def map_handed(slot):
+        @pl.when(is_handed(slot))
+        def _():
+            hand_copy(slot).wait_send()
+
+    same_side(map_handed)
 
     def sent(ahead, to):
         for phase in range(2):
-            out_copy(phase, me, to).wait_send()
-            back_copy(phase, me, to).wait_send()
+
+            @pl.when(me != ends[1 - phase])
+            def _():
+                out_copy(phase, me, to).wait_send()
+
+            @pl.when(to != ends[phase])
+            def _():
+                back_copy(phase, me, to).wait_send()
 
     others(sent)
     for which in range(3):
@@ -763,6 +795,7 @@
             dma((parts,)),
             dma((parts, groups // 2)),
             dma((parts, groups)),
+            pltpu.VMEM((groups // 2, channels, channels), f32),
         ],
         compiler_params=pltpu.CompilerParams(
             collective_id=0, has_side_effects=True, vmem_limit_bytes=61 << 20

time: 51.4 us -> 51 us (level)
    pallas_call x1, Pallas kernels: 48.9 us -> 48.3 us  [shards(): pl.pallas_call(functools.partial(kernel, dims), out_shape=(pltpu.VMEM((2,...]
where the time goes in v4:
time: 51 us; the launch traced here: 50.8 us
  Pallas kernels  50 us (98%)
  between operations  0.82 us (2%)
    pallas_call x1, Pallas kernels, shards(): pl.pallas_call(functools.partial(kernel, dims), out_shape=(pltpu.VMEM((2,...  48.3 us
    pallas_call x1, Pallas kernels, shards(): pl.pallas_call(write_out, out_shape=(jax.ShapeDtypeStruct((rows, channels...  1.6 us

profile of v4, /device:TPU:0, one launch (start us, length us, event | category | flops | bytes accessed | tf_op | source)
XLA Modules:
  0.0 50.8 jit_solution(6003019277670089051)
XLA Ops:
  0.6 48.3 %shard_map.75 = (f32[2,512,128]{2,1,0:T(8,128)S(1)}, f32[4,1152,128]{2,1,0:T(8,128)S(1)}, f32[4,128]{1,0:T(4,128)S(1)}) custom-call(f32[512,128]{1,0:T(8,128)} %bitcast.7, bf16[4,1152,128]{2,1,0:T(8,128)(2,1)} %bitcast.6, f32[4,128]{1,0:T(4,128)} %biases_in.1, f32[512,128]{1,0:T(8,128)} %bitcast.8), custom_call_target="tpu_custom_call" | custom-call | tf_op jit(solution)/shard_map/pallas_call | solution.py:750
  49.0 1.6 %shard_map.76 = (f32[512,128]{1,0:T(8,128)}, f32[512,128]{1,0:T(8,128)}, f32[4,1152,128]{2,1,0:T(8,128)}, f32[4,128]{1,0:T(4,128)}) custom-call(f32[2,512,128]{2,1,0:T(8,128)S(1)} %get-tuple-element.11.both, f32[4,1152,128]{2,1,0:T(8,128)S(1)} %get-tuple-element.12.wg, f32[4,128]{1,0:T(4,128)S(1)} %get-tuple-element.13.bg), custom_call_target="tpu_custom_call" | custom-call | tf_op jit(solution)/shard_map/pallas_call | solution.py:811

commit v5 on v4

--- a/solution.py
+++ b/solution.py
@@ -69,6 +69,12 @@
     spread_send,
     spread_recv,
     pair_maps,
+    pair_send,
+    pair_recv,
+    raw,
+    lent,
+    lend_send,
+    lend_recv,
 ):
     groups, parts, count, height, width, images_all = dims
     rows, channels = images_in.shape
@@ -134,42 +140,66 @@
 
         lax.fori_loop(1, groups // 2, step, 0)
 
-    def map_sends(body):
-        @pl.when(me < last)
+    odd = lax.rem(me, 2) == 1
+    pairs = groups // 2
+    mine = me // 2
+
+    def is_inner(m):
+        return (m > 0) & (m < pairs - 1)
+
+    def near_maps(body):
+        @pl.when(me != partner)
+        def _():
+            body(partner)
+
+        @pl.when(odd & (me < last))
         def _():
             body(after)
 
-        @pl.when(lax.rem(me, 2) == 1)
-        def _():
-            body(partner)
-
-        @pl.when(inner)
-        def _():
-            same_side(body)
-
-    map_sends(lambda to: map_copy(me, to).start())
-
-    def hand_copy(slot):
+    def far_maps(body):
+        @pl.when(jnp.logical_not(odd) & (me > 0))
+        def _():
+            body(before)
+
+    near_maps(lambda to: map_copy(me, to).start())
+
+    def pair_copy(m, to, sends):
         return pltpu.make_async_remote_copy(
-            src_ref=maps.at[slot],
-            dst_ref=maps.at[slot],
-            send_sem=hand_send.at[slot],
-            recv_sem=map_recv.at[slot],
-            device_id={"layer": partner},
+            src_ref=pair_maps.at[m],
+            dst_ref=pair_maps.at[m],
+            send_sem=sends,
+            recv_sem=pair_recv.at[m],
+            device_id={"layer": to},
             device_id_type=MESH,
         )
 
-    def is_handed(slot):
-        return (slot > 0) & (slot < last) & (slot + 1 != partner)
-
-    def hand_on(slot):
-        @pl.when((slot > 0) & (slot < last))
-        def _():
-            map_copy(slot, me).wait_recv()
-
-        @pl.when(is_handed(slot))
-        def _():
-            hand_copy(slot).start()
+    def pair_sends(body):
+        @pl.when(jnp.logical_not(odd) & is_inner(mine))
+        def _():
+            same_side(lambda to: body(pair_copy(mine, to, pair_send.at[to // 2])))
+
+    def other_pairs(body):
+        def step(m, _):
+            @pl.when(m != mine)
+            def _():
+                body(m)
+
+            return 0
+
+        lax.fori_loop(1, pairs - 1, step, 0)
+
+    def hand_pairs():
+        @pl.when(jnp.logical_not(odd))
+        def _():
+            def hand(m):
+                pair_copy(m, me, pair_send.at[m]).wait_recv()
+                pair_copy(m, partner, hand_send.at[m]).start()
+
+            other_pairs(hand)
+
+        @pl.when(odd)
+        def _():
+            other_pairs(lambda m: pair_copy(m, me, pair_send.at[m]).wait_recv())
 
     for load in loads[1:]:
         load.wait()
@@ -417,7 +447,7 @@
 
     def back_copy(phase, source, to):
         return pltpu.make_async_remote_copy(
-            src_ref=spread.at[phase, to],
+            src_ref=spread.at[phase, to // 2],
             dst_ref=error.at[phase, rows_of(source)],
             send_sem=back_send.at[phase, to],
             recv_sem=back_recv.at[phase, source],
@@ -425,75 +455,89 @@
             device_id_type=MESH,
         )
 
-    pairs = groups // 2
-    ends = (0, last)
+    def lend_copy(phase):
+        return pltpu.make_async_remote_copy(
+            src_ref=raw,
+            dst_ref=lent.at[phase],
+            send_sem=lend_send.at[phase],
+            recv_sem=lend_recv.at[phase],
+            device_id={"layer": partner},
+            device_id_type=MESH,
+        )
+
+    steps = (apply_map, apply_flipped)
+    first_pair = (0, pairs - 1)
 
     def chain_start(phase, value):
-        residue[phase] = value
-
-        @pl.when(me != ends[1 - phase])
+        leads = takes(phase)
+
+        @pl.when(leads)
+        def _():
+            residue[phase] = steps[phase](value, partner)
+
+        @pl.when(jnp.logical_not(leads))
+        def _():
+            residue[phase] = value
+
+        @pl.when(mine != first_pair[1 - phase])
         def _():
             others(lambda ahead, to: out_copy(phase, me, to).start())
 
         gathered[phase, me] = residue[phase, rows_of(me)]
 
-    def pair_up(m, _):
-        one = maps[2 * m]
-        two = maps[2 * m + 1]
-        pair_maps[m] = one + two + dot(one.astype(low), two.astype(low))
-        return 0
+        @pl.when(leads)
+        def _():
+            raw[...] = value
+            lend_copy(phase).start()
 
     def chain_scan(phase):
-        apply = apply_map if phase == 0 else apply_flipped
-
-        def deliver(k, value):
-            @pl.when(k != me)
-            def _():
-                spread[phase, k] = value
-                back_copy(phase, me, k).start()
-
-            @pl.when(k == me)
+        def deliver(m, value):
+            spread[phase, m] = value
+
+            for k in (2 * m, 2 * m + 1):
+
+                @pl.when(k != me)
+                def _():
+                    back_copy(phase, me, k).start()
+
+            @pl.when(m == mine)
             def _():
                 error[phase, rows_of(me)] = value
 
-        def arrived(k):
-            @pl.when(k != me)
-            def _():
-                out_copy(phase, k, me).wait_recv()
+        def both(m):
+            for k in (2 * m, 2 * m + 1):
+
+                @pl.when(k != me)
+                def _():
+                    out_copy(phase, k, me).wait_recv()
+
+            return gathered[phase, 2 * m] + gathered[phase, 2 * m + 1]
 
         def pair_of(i):
-            m = i if phase == 0 else pairs - 1 - i
-            return 2 * m + phase, 2 * m + 1 - phase, m
+            return i if phase == 0 else pairs - 1 - i
 
         def step(i, carried):
-            one, two, m = pair_of(i)
-            deliver(one, carried)
-            moved = apply(carried, one)
-            jumped = apply(carried, m, pair_maps)
-            arrived(one)
-            deliver(two, moved + gathered[phase, one])
-            jumped = jumped + apply(gathered[phase, one], two)
-            arrived(two)
-            return jumped + gathered[phase, two]
-
-        one, two, _ = pair_of(0)
-        arrived(one)
-        deliver(two, gathered[phase, one])
-        carried = apply(gathered[phase, one], two)
-        arrived(two)
-        carried = lax.fori_loop(1, pairs - 1, step, carried + gathered[phase, two])
-        one, two, _ = pair_of(pairs - 1)
-        deliver(one, carried)
-        moved = apply(carried, one)
-        arrived(one)
-        deliver(two, moved + gathered[phase, one])
+            m = pair_of(i)
+            deliver(m, carried)
+            moved = steps[phase](carried, m, pair_maps)
+            return moved + both(m)
+
+        carried = lax.fori_loop(1, pairs - 1, step, both(pair_of(0)))
+        deliver(pair_of(pairs - 1), carried)
 
     def chain_finish(phase):
-        @pl.when(me != ends[phase])
+        @pl.when(mine != first_pair[phase])
         def _():
             others(lambda ahead, to: back_copy(phase, to, me).wait_recv())
 
-        return jnp.where(me == ends[phase], 0.0, error[phase])
+        leads = takes(phase)
+
+        @pl.when(jnp.logical_not(leads))
+        def _():
+            lend_copy(phase).wait_recv()
+
+        value = jnp.where(mine == first_pair[phase], 0.0, error[phase])
+        return jnp.where(leads, value, steps[phase](value, partner) + lent[phase])
 
     def nth_other(i):
         back_side = parts - 1 - z
@@ -570,32 +614,42 @@
 
     start_image = part_images[z]
 
-    @pl.when(me != 0)
+    def wait_before():
+        @pl.when(me > 0)
+        def _():
+            map_copy(before, me).wait_recv()
+
+    def wait_after():
+        @pl.when(me < last)
+        def _():
+            map_copy(after, me).wait_recv()
+
+    def join_pair():
+        one = maps[2 * mine]
+        two = maps[2 * mine + 1]
+        pair_maps[mine] = one + two + dot(one.astype(low), two.astype(low))
+
+    @pl.when(jnp.logical_not(odd))
     def _():
-        map_copy(before, me).wait_recv()
-
+        wait_after()
+        join_pair()
+
+    pair_sends(lambda copy: copy.start())
+    wait_before()
     starts = start_of(start_image)
     chain_start(0, relax(starts) - apply_map(start_image, me))
 
-    same_side(hand_on)
-
-    def wait_map(ahead, source):
-        across = lax.rem(source - me + groups, 2) != 0
-        sent = (source > 0) & ((source < last) | (me == last - 1))
-
-        @pl.when(across & sent & (source != me - 1))
-        def _():
-            map_copy(source, me).wait_recv()
-
-    others(wait_map)
-    lax.fori_loop(1, pairs - 1, pair_up, 0)
+    far_maps(lambda to: map_copy(me, to).start())
+
+    @pl.when(odd)
+    def _():
+        join_pair()
+
+    hand_pairs()
 
     def ends_of(field):
         return jnp.where(me == last, field, apply_flipped(field, after))
 
-    end = end_grad[...]
-    ends_adj = ends_of(end)
-    back = apply_flipped(end, me)
     others_count = parts - 1
 
     def images_on(i):
@@ -625,6 +679,14 @@
         share_on(i)
     images_on(0)
     relax_on(0)
+
+    @pl.when(odd)
+    def _():
+        wait_after()
+
+    end = end_grad[...]
+    ends_adj = ends_of(end)
+    back = apply_flipped(end, me)
     corrected = starts + chain_finish(0)
     states_all[z] = corrected
     line_start(0)
@@ -641,7 +703,6 @@
     relax_on(2)
     states_on(1)
     follow(1)
-    answer(1)
     adjoint = ends_adj + chain_finish(1)
     adj_all[z] = adjoint
     line_start(1)
@@ -657,40 +718,52 @@
     late = range(count // 2, count)
     if parts > 1:
         line_round(1, 1, early)
-    for i in range(2, others_count):
-        answer(i)
+        pass_on(1, 0, early)
+        answer(1)
     for i in range(others_count):
-        pass_on(1, i, early)
         line_round(1, i + 1, late)
         pass_on(1, i, late)
+        part = nth_other(i)
         if i < others_count - 1:
             pass_wait(1, i)
-            part = nth_other(i)
             sweep(part, adj_all[part])
             line_round(1, i + 2, early)
+            pass_on(1, i + 1, early)
+            answer(i + 2)
         else:
-            part = nth_other(i)
-            for at in range(count):
-                pass_wait(1, i, (at,))
-                sweep(part, adj_all[part, at * piece : (at + 1) * piece], at)
-
-    map_sends(lambda to: map_copy(me, to).wait_send())
-
-    def map_handed(slot):
-        @pl.when(is_handed(slot))
-        def _():
-            hand_copy(slot).wait_send()
-
-    same_side(map_handed)
+
+            @pl.when(jnp.logical_not(lead))
+            def _():
+                sweep(part, adj_all[part])
+
+            @pl.when(lead)
+            def _():
+                for at in range(count):
+                    pass_wait(1, i, (at,))
+                    sweep(part, adj_all[part, at * piece : (at + 1) * piece], at)
+
+    near_maps(lambda to: map_copy(me, to).wait_send())
+    far_maps(lambda to: map_copy(me, to).wait_send())
+    pair_sends(lambda copy: copy.wait_send())
+
+    @pl.when(jnp.logical_not(odd))
+    def _():
+        other_pairs(lambda m: pair_copy(m, partner, hand_send.at[m]).wait_send())
+
+    for phase in range(2):
+
+        @pl.when(takes(phase))
+        def _():
+            lend_copy(phase).wait_send()
 
     def sent(ahead, to):
         for phase in range(2):
 
-            @pl.when(me != ends[1 - phase])
+            @pl.when(mine != first_pair[1 - phase])
             def _():
                 out_copy(phase, me, to).wait_send()
 
-            @pl.when(to != ends[phase])
+            @pl.when(to // 2 != first_pair[phase])
             def _():
                 back_copy(phase, me, to).wait_send()
 
@@ -796,6 +869,12 @@
             dma((parts, groups // 2)),
             dma((parts, groups)),
             pltpu.VMEM((groups // 2, channels, channels), f32),
+            dma((groups // 2,)),
+            dma((groups // 2,)),
+            pltpu.VMEM((rows, channels), f32),
+            pltpu.VMEM((2, rows, channels), f32),
+            dma((2,)),
+            dma((2,)),
         ],
         compiler_params=pltpu.CompilerParams(
             collective_id=0, has_side_effects=True, vmem_limit_bytes=61 << 20

time: 51 us -> 51 us (level)
  no operation moved by 1% of the time
where the time goes in v5:
time: 51 us; the launch traced here: 50.8 us
  Pallas kernels  50 us (98%)
  between operations  0.82 us (2%)
    pallas_call x1, Pallas kernels, shards(): pl.pallas_call(functools.partial(kernel, dims), out_shape=(pltpu.VMEM((2,...  48.4 us
    pallas_call x1, Pallas kernels, shards(): pl.pallas_call(write_out, out_shape=(jax.ShapeDtypeStruct((rows, channels...  1.6 us

profile of v5, /device:TPU:0, one launch (start us, length us, event | category | flops | bytes accessed | tf_op | source)
XLA Modules:
  0.0 50.8 jit_solution(17067760289339052570)
XLA Ops:
  0.6 48.4 %shard_map.75 = (f32[2,512,128]{2,1,0:T(8,128)S(1)}, f32[4,1152,128]{2,1,0:T(8,128)S(1)}, f32[4,128]{1,0:T(4,128)S(1)}) custom-call(f32[512,128]{1,0:T(8,128)} %bitcast.7, bf16[4,1152,128]{2,1,0:T(8,128)(2,1)} %bitcast.6, f32[4,128]{1,0:T(4,128)} %biases_in.1, f32[512,128]{1,0:T(8,128)} %bitcast.8), custom_call_target="tpu_custom_call" | custom-call | tf_op jit(solution)/shard_map/pallas_call | solution.py:823
  49.0 1.6 %shard_map.76 = (f32[512,128]{1,0:T(8,128)}, f32[512,128]{1,0:T(8,128)}, f32[4,1152,128]{2,1,0:T(8,128)}, f32[4,128]{1,0:T(4,128)}) custom-call(f32[2,512,128]{2,1,0:T(8,128)S(1)} %get-tuple-element.11.both, f32[4,1152,128]{2,1,0:T(8,128)S(1)} %get-tuple-element.12.wg, f32[4,128]{1,0:T(4,128)S(1)} %get-tuple-element.13.bg), custom_call_target="tpu_custom_call" | custom-call | tf_op jit(solution)/shard_map/pallas_call | solution.py:890

commit v6 on v5

--- a/solution.py
+++ b/solution.py
@@ -324,7 +324,6 @@
         back_edge[n, spot(1), spot(0)] = nothing
         back_edge[n, spot(0), spot(1)] = tap(1, 0)
         back_edge[n, spot(1), spot(1)] = tap(0, 0)
-        wg_out[n] = jnp.zeros(wg_out.shape[1:], jnp.float32)
         return 0
 
     lax.fori_loop(0, blocks, prepare, 0)
@@ -413,7 +412,7 @@
 
     divisor = 1.0 / images_all
 
-    def sweep(part, adjoint, first=0):
+    def sweep(part, adjoint, first=0, fresh=False):
         def step(i, adjoints):
             n = blocks - 1 - i
             after = []
@@ -428,9 +427,9 @@
             used = states_low[n, part, first * area : (first + len(spots)) * area]
             grads = dot(used, join(spots), TN) * divisor
             for tap in range(9):
-                wg_out[n, (8 - tap) * channels : (9 - tap) * channels, :] += grads[
-                    :, tap * channels : (tap + 1) * channels
-                ]
+                place = slice((8 - tap) * channels, (9 - tap) * channels)
+                grad = grads[:, tap * channels : (tap + 1) * channels]
+                wg_out[n, place, :] = grad if fresh else wg_out[n, place, :] + grad
             return tuple(after)
 
         return join(lax.fori_loop(0, blocks, step, split(adjoint), unroll=4))
@@ -711,7 +710,7 @@
             images_on(i)
             relax_on(i)
         states_on(i)
-    both_out[1] = sweep(z, adjoint)
+    both_out[1] = sweep(z, adjoint, fresh=True)
     for i in range(2, others_count):
         follow(i)
     early = range(count // 2)

time: 51 us -> 51 us (level)
  no operation moved by 1% of the time
where the time goes in v6:
time: 51 us; the launch traced here: 50.8 us
  Pallas kernels  50 us (98%)
  between operations  0.82 us (2%)
    pallas_call x1, Pallas kernels, shards(): pl.pallas_call(functools.partial(kernel, dims), out_shape=(pltpu.VMEM((2,...  48.4 us
    pallas_call x1, Pallas kernels, shards(): pl.pallas_call(write_out, out_shape=(jax.ShapeDtypeStruct((rows, channels...  1.6 us

profile of v6, /device:TPU:0, one launch (start us, length us, event | category | flops | bytes accessed | tf_op | source)
XLA Modules:
  0.0 50.8 jit_solution(6923742137710887458)
XLA Ops:
  0.6 48.4 %shard_map.75 = (f32[2,512,128]{2,1,0:T(8,128)S(1)}, f32[4,1152,128]{2,1,0:T(8,128)S(1)}, f32[4,128]{1,0:T(4,128)S(1)}) custom-call(f32[512,128]{1,0:T(8,128)} %bitcast.7, bf16[4,1152,128]{2,1,0:T(8,128)(2,1)} %bitcast.6, f32[4,128]{1,0:T(4,128)} %biases_in.1, f32[512,128]{1,0:T(8,128)} %bitcast.8), custom_call_target="tpu_custom_call" | custom-call | tf_op jit(solution)/shard_map/pallas_call | solution.py:822
  49.0 1.6 %shard_map.76 = (f32[512,128]{1,0:T(8,128)}, f32[512,128]{1,0:T(8,128)}, f32[4,1152,128]{2,1,0:T(8,128)}, f32[4,128]{1,0:T(4,128)}) custom-call(f32[2,512,128]{2,1,0:T(8,128)S(1)} %get-tuple-element.11.both, f32[4,1152,128]{2,1,0:T(8,128)S(1)} %get-tuple-element.12.wg, f32[4,128]{1,0:T(4,128)S(1)} %get-tuple-element.13.bg), custom_call_target="tpu_custom_call" | custom-call | tf_op jit(solution)/shard_map/pallas_call | solution.py:889
